TPU v7x, 32 devices: a whole 2x2x4 slice. The times are simulated.
32 devices in a mesh: frames: 4 (over y, x), tiles: 8 (over z, core).
Axes of the slice: x: 2, y: 2, z: 4, core: 2. Of those that a mesh axis runs over, the one named last changes fastest.
Arguments:
- features: bfloat16 [16, 64, 480, 128], P('frames', 'tiles'), may hold values from -6 to 6
- w_conv: bfloat16 [3, 3, 128, 128], replicated, may hold values from -0.1875 to 0.1875
- query_feats: bfloat16 [4096, 128], P(('frames', 'tiles')), may hold values from -6 to 6
- offset_rows: int32 [16, 32], P('frames'), may hold values from 0 to 7
- offset_cols: int32 [16, 32], P('frames'), may hold values from 0 to 471
- owners: int32 [32, 1], replicated, may hold values from 0 to 7; in each aligned block of 32 rows (0 to 31, 32 to 63, ...) at most 12 rows name the same one
- start_frames: int32 [4096], P(('frames', 'tiles')), may hold values from 0 to 15
- w_corr: bfloat16 [81, 384], replicated, may hold values from -0.625 to 0.625
- w_feat: bfloat16 [128, 384], replicated, may hold values from -0.5 to 0.5
- time_embed: float32 [16, 384], replicated, may hold values from -3 to 3
- gain_attn: float32 [384], replicated, may hold values from 0.5 to 1.5
- w_qkv: bfloat16 [384, 1152], replicated, may hold values from -1.0716518 to 1.0716518
- w_attn_out: bfloat16 [384, 384], replicated, may hold values from -0.3125 to 0.3125
- gain_mlp: float32 [384], replicated, may hold values from 0.5 to 1.5
- w_up: bfloat16 [384, 1536], replicated, may hold values from -0.3125 to 0.3125
- w_down: bfloat16 [1536, 384], replicated, may hold values from -0.15625 to 0.15625
Outputs:
- refined: bfloat16 [4096, 16, 384], P(('frames', 'tiles'))
Inputs may be any that keep to these rules, and one draw needn't show every extreme that they name: `owners`: no tile owns more than 12 query blocks; some tile owns exactly 12; every tile owns at least one.
All inputs are finite; a program needn't handle non-finite values.
Results may differ from a plain program's by a relative error of at most 0.0066.
Values may be sent and summed in bfloat16 or wider, within the bound.
A program may use at most 192 MiB of HBM per device.

v0:
```python
import jax
import jax.numpy as jnp
from jax import lax
from jax.sharding import PartitionSpec as P

HEADS = 8
WIN = 9
QBLK = 128


def extended_2(cells, sides, width):
    for axis, dim in sides:
        count = lax.axis_size(axis)
        ends = count - 1
        head = lax.slice_in_dim(cells, 0, width, axis=dim)
        tail = lax.slice_in_dim(cells, cells.shape[dim] - width, cells.shape[dim], axis=dim)
        cells = jnp.concatenate(
            [
                lax.ppermute(tail, axis, [(i, (i + 1) % count) for i in range(ends)]),
                cells,
                lax.ppermute(head, axis, [((i + 1) % count, i) for i in range(ends)]),
            ],
            axis=dim,
        )
    return cells


def from_partner(value, axis, apart):
    mask = 2**apart
    pairs = [(source, source ^ mask) for source in range(lax.axis_size(axis))]
    return lax.ppermute(value, axis, pairs)


def convolve(padded, w_conv, out_rows):
    frames, rows, cols, chans = padded.shape
    wide = jnp.pad(padded, ((0, 0), (0, 0), (1, 1), (0, 0)))
    total = jnp.zeros((frames, out_rows, cols, chans), jnp.float32)
    for a in range(3):
        for b in range(3):
            total = total + jnp.einsum(
                "fhwc,cd->fhwd",
                wide[:, a : a + out_rows, b : b + cols],
                w_conv[a, b],
                preferred_element_type=jnp.float32,
            )
    return total.astype(jnp.bfloat16)


def rms_scale(values, gain):
    return values * lax.rsqrt(jnp.mean(values * values, axis=-1, keepdims=True) + 1e-06) * gain


def token_layer(tokens, starts, gain_attn, w_qkv, w_attn_out, gain_mlp, w_up, w_down):
    tracks, frames, width = tokens.shape
    head = width // HEADS
    normed = rms_scale(tokens, gain_attn).astype(jnp.bfloat16)
    qkv = jnp.einsum("tfd,de->tfe", normed, w_qkv, preferred_element_type=jnp.float32).astype(
        jnp.bfloat16
    )
    query = qkv[..., :width].reshape(tracks, frames, HEADS, head)
    keys = qkv[..., width : 2 * width].reshape(tracks, frames, HEADS, head)
    values = qkv[..., 2 * width :].reshape(tracks, frames, HEADS, head)
    scores = jnp.einsum(
        "tfhe,tghe->thfg", query, keys, preferred_element_type=jnp.float32
    ) * head ** (-0.5)
    valid = jnp.arange(frames)[None, :] >= starts[:, None]
    scores = jnp.where(valid[:, None, None, :], scores, -1e30)
    top = jnp.max(scores, axis=-1, keepdims=True)
    weights = jnp.exp(scores - top)
    probs = (weights / jnp.sum(weights, axis=-1, keepdims=True)).astype(jnp.bfloat16)
    attended = jnp.einsum(
        "thfg,tghe->tfhe", probs, values, preferred_element_type=jnp.float32
    ).astype(jnp.bfloat16)
    attended = attended.reshape(tracks, frames, width)
    mixed = tokens + jnp.einsum(
        "tfd,de->tfe", attended, w_attn_out, preferred_element_type=jnp.float32
    )
    normed2 = rms_scale(mixed, gain_mlp).astype(jnp.bfloat16)
    hidden = jax.nn.gelu(
        jnp.einsum("tfd,de->tfe", normed2, w_up, preferred_element_type=jnp.float32),
        approximate=True,
    ).astype(jnp.bfloat16)
    result = mixed + jnp.einsum("tfe,ed->tfd", hidden, w_down, preferred_element_type=jnp.float32)
    return result.astype(jnp.bfloat16)


def body(
    features,
    w_conv,
    query_feats,
    offset_rows,
    offset_cols,
    owners,
    start_frames,
    w_corr,
    w_feat,
    time_embed,
    gain_attn,
    w_qkv,
    w_attn_out,
    gain_mlp,
    w_up,
    w_down,
):
    n_tiles = lax.axis_size("tiles")
    n_frames = lax.axis_size("frames")
    tile = lax.axis_index("tiles")
    frame_dev, rows, width, chans = features.shape
    padded = extended_2(features, (("tiles", 1),), 1)
    conv = convolve(padded, w_conv, rows)
    extended = extended_2(conv, (("tiles", 1),), 4)
    all_queries = lax.all_gather(query_feats, ("frames", "tiles"), axis=0, tiled=True).reshape(
        -1, QBLK, chans
    )
    blocks = all_queries.shape[0]
    blk_dev = blocks // (n_frames * n_tiles)
    per_group = blocks // n_frames
    scale = chans ** (-0.5)

    def frame_patch(frame, row, col):
        zero_start = jnp.zeros((), jnp.int32)
        return lax.dynamic_slice(frame, (row, col, zero_start), (WIN, WIN, chans)).reshape(
            WIN * WIN, chans
        )

    capacity = 3 * blocks // n_tiles
    refined_count = blocks // n_tiles
    levels = n_tiles.bit_length() - 1
    tile_list = jnp.arange(n_tiles, dtype=jnp.int32)

    def initial_ids(tile_here):
        foreign = (owners[:, 0] != tile_here).astype(jnp.int32)
        order = jnp.argsort(foreign, stable=True)[:capacity]
        return jnp.where(owners[order, 0] == tile_here, order, -1)

    ids_all = jax.vmap(initial_ids)(tile_list)
    own_ids = ids_all[tile]
    live = (own_ids >= 0).astype(jnp.bfloat16)
    block_ids = jnp.maximum(own_ids, 0)
    chosen = all_queries[block_ids]
    row_sel = offset_rows[:, block_ids].T
    col_sel = offset_cols[:, block_ids].T
    patches = jax.vmap(lambda rr, cc: jax.vmap(frame_patch)(extended, rr, cc))(row_sel, col_sel)
    corr = jnp.einsum("mfkc,mqc->mfkq", patches, chosen, preferred_element_type=jnp.float32) * scale
    held_rows = corr.astype(jnp.bfloat16) * live[:, None, None, None]
    size_now = capacity
    for level in range(levels):
        size_next = min(capacity * 2 ** (level + 1), refined_count * 2 ** (levels - level - 1))
        send_size = min(size_now, size_next)

        def split(id_row, tile_here):
            own_bit = jnp.right_shift(tile_here, level) & 1
            dest_bit = jnp.right_shift(id_row % per_group // blk_dev, level) & 1
            going = (id_row >= 0) & (dest_bit != own_bit)
            order = jnp.argsort(jnp.where(going, 0, 1).astype(jnp.int32), stable=True)[:send_size]
            sent = jnp.where(going[order], id_row[order], -1)
            kept = jnp.where(going, -1, id_row)
            return (order, sent, kept)

        orders, sent_all, kept_all = jax.vmap(split)(ids_all, tile_list)
        partner = jnp.bitwise_xor(tile_list, 1 << level)
        merged_all = jnp.concatenate([kept_all, sent_all[partner]], axis=1)

        def compact(id_row):
            order = jnp.argsort(jnp.where(id_row >= 0, 0, 1).astype(jnp.int32), stable=True)[
                :size_next
            ]
            return (order, id_row[order])

        picks, ids_all = jax.vmap(compact)(merged_all)
        outgoing = held_rows[orders[tile]]
        incoming = from_partner(outgoing, "tiles", level)
        pooled = jnp.concatenate([held_rows, incoming], axis=0)
        held_rows = pooled[picks[tile]]
        size_now = size_next
    final_ids = ids_all[tile]
    position = final_ids // per_group * blk_dev + final_ids % per_group % blk_dev
    placement = jnp.argsort(position)
    shares = held_rows[placement].reshape(1, n_frames, blk_dev, frame_dev, WIN * WIN, QBLK)
    arrived = lax.all_to_all(shares, "frames", split_axis=1, concat_axis=3, tiled=True)
    frames_total = frame_dev * n_frames
    corr_dev = arrived.reshape(blk_dev, frames_total, WIN * WIN, QBLK)
    tokens = jnp.einsum("bfkq,kd->bqfd", corr_dev, w_corr, preferred_element_type=jnp.float32)
    feat_proj = jnp.dot(query_feats, w_feat, preferred_element_type=jnp.float32).reshape(
        blk_dev, QBLK, 1, -1
    )
    tokens = tokens + feat_proj + time_embed[None, None]
    tokens = tokens.reshape(blk_dev * QBLK, frames_total, -1)
    return token_layer(tokens, start_frames, gain_attn, w_qkv, w_attn_out, gain_mlp, w_up, w_down)


def solution(mesh):
    placed = (
        P("frames", "tiles", None, None),
        P(),
        P(("frames", "tiles"), None),
        P("frames", None),
        P("frames", None),
        P(),
        P(("frames", "tiles")),
        P(),
        P(),
        P(),
        P(),
        P(),
        P(),
        P(),
        P(),
        P(),
    )
    return jax.shard_map(
        body,
        mesh=mesh,
        in_specs=placed,
        out_specs=P(("frames", "tiles"), None, None),
        check_vma=False,
    )
```

profile of v0, /device:TPU:0, one launch (start us, length us, event | category | flops | bytes accessed | tf_op | source)
XLA Modules:
  0.0 315.9 jit_solution(12538587905631740332)
XLA Ops:
  27.2 6.6 %fusion.69 = f32[4,8,480,128]{3,2,1,0:T(8,128)} fusion(bf16[4,8,480,128]{3,2,1,0:T(8,128)(2,1)} %param.16, bf16[3,3,128,128]{3,2,1,0:T(8,128)(2,1)S(1)} %copy-done.6), kind=kOutput, calls=%fused_computation.107 | convolution fusion | flops 503316480 | bytes 11829248 | tf_op jit(solution)/shard_map/fhwc,cd->fhwd/dot_general | solution.py:40
  33.9 3.6 %fusion.14 = bf16[4,10,482,128]{3,2,1,0:T(8,128)(2,1)S(1)} fusion(bf16[4,1,480,128]{3,2,1,0:T(8,128)(2,1)S(1)} %collective-permute-done.1, bf16[4,8,480,128]{3,2,1,0:T(8,128)(2,1)S(1)} %copy-done.3, bf16[4,1,480,128]{3,2,1,0:T(8,128)(2,1)S(1)} %collective-permute-done), kind=kLoop, calls=%fused_computation.44 | loop fusion | flops 29614080 | bytes 9850880 | tf_op jit(solution)/shard_map/concatenate | solution.py:17
  37.5 4.7 %fusion.25 = f32[4,8,480,128]{3,2,1,0:T(8,128)} fusion(bf16[4,10,482,128]{3,2,1,0:T(8,128)(2,1)S(1)} %fusion.14, bf16[3,3,128,128]{3,2,1,0:T(8,128)(2,1)S(1)} %copy-done.6), kind=kOutput, calls=%fused_computation.56 | convolution fusion | flops 503316480 | bytes 11829248 | tf_op jit(solution)/shard_map/fhwc,cd->fhwd/dot_general | solution.py:40
  42.1 4.3 %fusion.27 = f32[4,8,480,128]{3,2,1,0:T(8,128)} fusion(bf16[4,10,482,128]{3,2,1,0:T(8,128)(2,1)S(1)} %fusion.14, bf16[3,3,128,128]{3,2,1,0:T(8,128)(2,1)S(1)} %copy-done.6), kind=kOutput, calls=%fused_computation.58 | convolution fusion | flops 503316480 | bytes 11829248 | tf_op jit(solution)/shard_map/fhwc,cd->fhwd/dot_general | solution.py:40
  46.4 4.3 %fusion.29 = f32[4,8,480,128]{3,2,1,0:T(8,128)} fusion(bf16[4,10,482,128]{3,2,1,0:T(8,128)(2,1)S(1)} %fusion.14, bf16[3,3,128,128]{3,2,1,0:T(8,128)(2,1)S(1)} %copy-done.6), kind=kOutput, calls=%fused_computation.60 | convolution fusion | flops 503316480 | bytes 11829248 | tf_op jit(solution)/shard_map/fhwc,cd->fhwd/dot_general | solution.py:40
  50.7 4.3 %fusion.31 = f32[4,8,480,128]{3,2,1,0:T(8,128)} fusion(bf16[4,10,482,128]{3,2,1,0:T(8,128)(2,1)S(1)} %fusion.14, bf16[3,3,128,128]{3,2,1,0:T(8,128)(2,1)S(1)} %copy-done.6), kind=kOutput, calls=%fused_computation.62 | convolution fusion | flops 503316480 | bytes 11829248 | tf_op jit(solution)/shard_map/fhwc,cd->fhwd/dot_general | solution.py:40
  55.1 4.3 %fusion.33 = f32[4,8,480,128]{3,2,1,0:T(8,128)} fusion(bf16[4,10,482,128]{3,2,1,0:T(8,128)(2,1)S(1)} %fusion.14, bf16[3,3,128,128]{3,2,1,0:T(8,128)(2,1)S(1)} %copy-done.6), kind=kOutput, calls=%fused_computation.64 | convolution fusion | flops 503316480 | bytes 11829248 | tf_op jit(solution)/shard_map/fhwc,cd->fhwd/dot_general | solution.py:40
  59.4 4.2 %fusion.15 = f32[4,8,480,128]{3,2,1,0:T(8,128)} fusion(bf16[4,8,480,128]{3,2,1,0:T(8,128)(2,1)S(1)} %copy-done.3, bf16[4,1,480,128]{3,2,1,0:T(8,128)(2,1)S(1)} %collective-permute-done, bf16[3,3,128,128]{3,2,1,0:T(8,128)(2,1)S(1)} %copy-done.6), kind=kOutput, calls=%fused_computation.45 | convolution fusion | flops 512163840 | bytes 12320768 | tf_op jit(solution)/shard_map/fhwc,cd->fhwd/dot_general | solution.py:40
  63.6 4.2 %fusion.19 = f32[4,8,480,128]{3,2,1,0:T(8,128)} fusion(bf16[4,1,480,128]{3,2,1,0:T(8,128)(2,1)S(1)} %collective-permute-done.1, bf16[4,8,480,128]{3,2,1,0:T(8,128)(2,1)S(1)} %copy-done.3, bf16[3,3,128,128]{3,2,1,0:T(8,128)(2,1)S(1)} %copy-done.6), kind=kOutput, calls=%fused_computation.49 | convolution fusion | flops 512163840 | bytes 12320768 | tf_op jit(solution)/shard_map/fhwc,cd->fhwd/dot_general | solution.py:40
  67.9 23.6 %add_convert_fusion = bf16[4,8,480,128]{3,2,1,0:T(8,128)(2,1)} fusion(f32[4,8,480,128]{3,2,1,0:T(8,128)} %fusion.19, f32[4,8,480,128]{3,2,1,0:T(8,128)} %fusion.25, f32[4,8,480,128]{3,2,1,0:T(8,128)} %fusion.27, f32[4,8,480,128]{3,2,1,0:T(8,128)} %fusion.69, f32[4,8,480,128]{3,2,1,0:T(8,128)} %fusion.29, f32[4,8,480,128]{3,2,1,0:T(8,128)} %fusion.31, ...), kind=kOutput, calls=%fused_computation.38 | convolution fusion | flops 521011200 | bytes 70811648 | tf_op jit(solution)/shard_map/fhwc,cd->fhwd/dot_general | solution.py:40
  91.5 4.3 %fusion.158 = (bf16[4,4,480,128]{3,2,1,0:T(8,128)(2,1)}, bf16[4,4,480,128]{3,2,1,0:T(8,128)(2,1)}) fusion(bf16[4,8,480,128]{3,2,1,0:T(8,128)(2,1)} %add_convert_fusion), kind=kLoop, calls=%fused_computation.272 | loop fusion | bytes 7864320 | tf_op jit(solution)/shard_map/slice | solution.py:16
  95.8 5.3 %collective-permute-start.2 = (bf16[4,4,480,128]{3,2,1,0:T(8,128)(2,1)}, bf16[4,4,480,128]{3,2,1,0:T(8,128)(2,1)S(1)}, u32[]{:S(2)}, u32[]{:S(2)}) collective-permute-start(bf16[4,4,480,128]{3,2,1,0:T(8,128)(2,1)} %get-tuple-element.37), channel_id=1, source_target_pairs={{0,1},{1,2},{2,3},{3,4},{4,5},{5,6},{6,7},{8,9},{9,10},{10,11},{11... | collective-permute-start | bytes 5898248 | tf_op jit(solution)/shard_map/ppermute | solution.py:19
  110.2 6.5 %pad_maximum_fusion = bf16[4,16,480,128]{3,2,1,0:T(8,128)(2,1)} fusion(bf16[4,4,480,128]{3,2,1,0:T(8,128)(2,1)} %collective-permute-done.3, bf16[4,8,480,128]{3,2,1,0:T(8,128)(2,1)} %add_convert_fusion, bf16[4,4,480,128]{3,2,1,0:T(8,128)(2,1)S(1)} %collective-permute-done.2), kind=kLoop, calls=%fused_computation.37 | loop fusion | flops 7864320 | bytes 15728640 | tf_op jit(solution)/shard_map/concatenate | solution.py:17
  116.7 12.5 %copy.139 = bf16[4,16,480,128]{3,0,2,1:T(4,128)(2,1)} copy(bf16[4,16,480,128]{3,2,1,0:T(8,128)(2,1)} %pad_maximum_fusion) | data formatting | bytes 15728640 | tf_op jit(solution)/shard_map/concatenate | solution.py:17
  129.2 6.7 %gather_fusion.14 = bf16[48,9,9,128]{3,0,2,1:T(8,128)(2,1)S(1)} fusion(bf16[4,16,480,128]{3,0,2,1:T(4,128)(2,1)} %copy.139, s32[48]{0:T(128)S(1)} %reshape.452), kind=kCustom, calls=%fused_computation.14 | custom fusion | bytes 1991424 | tf_op jit(solution)/shard_map/vmap(vmap())/gather | solution.py:122
  139.7 18.8 %collective-permute-start.4 = (bf16[12,4,81,128]{3,1,2,0:T(4,128)(2,1)}, bf16[12,4,81,128]{3,1,2,0:T(4,128)(2,1)S(1)}, u32[]{:S(2)}, u32[]{:S(2)}) collective-permute-start(bf16[12,4,81,128]{3,1,2,0:T(4,128)(2,1)} %copy.142), channel_id=1, source_target_pairs={{0,1},{1,0},{2,3},{3,2},{4,5},{5,4},{6,7},{7,6},{8,9},{9,8},{10,11... | collective-permute-start | bytes 2985992 | tf_op jit(solution)/shard_map/ppermute | solution.py:31
  167.9 15.6 %collective-permute-done.5 = bf16[8,4,81,128]{3,0,2,1:T(8,128)(2,1)S(1)} collective-permute-done((bf16[8,4,81,128]{3,0,2,1:T(8,128)(2,1)S(1)}, bf16[8,4,81,128]{3,0,2,1:T(8,128)(2,1)S(1)}, u32[]{:S(2)}, u32[]{:S(2)}) %collective-permute-start.5) | collective-permute-done | bytes 663584 | tf_op jit(solution)/shard_map/ppermute | solution.py:31
  190.7 15.9 %collective-permute-done.6 = bf16[4,4,81,128]{3,2,1,0:T(8,128)(2,1)S(1)} collective-permute-done((bf16[4,4,81,128]{3,2,1,0:T(8,128)(2,1)S(1)}, bf16[4,4,81,128]{3,2,1,0:T(8,128)(2,1)S(1)}, u32[]{:S(2)}, u32[]{:S(2)}) %collective-permute-start.6) | collective-permute-done | bytes 331808 | tf_op jit(solution)/shard_map/ppermute | solution.py:31
  208.9 3.8 %all-to-all-start = ((bf16[1,4,1,4,81,128]{5,3,4,2,0,1:T(4,128)(2,1)}), bf16[1,4,1,4,81,128]{5,3,4,2,0,1:T(4,128)(2,1)S(1)}, u32[]{:S(2)}, u32[]{:S(2)}) async-start(bf16[1,4,1,4,81,128]{5,3,4,2,0,1:T(4,128)(2,1)} %copy.159), calls=%async_computation | async-start | bytes 663552 | tf_op jit(solution)/shard_map/all_to_all | solution.py:180
  212.9 5.4 %all-to-all-done = bf16[1,4,1,4,81,128]{5,3,4,2,0,1:T(4,128)(2,1)S(1)} async-done(((bf16[1,4,1,4,81,128]{5,3,4,2,0,1:T(4,128)(2,1)}), bf16[1,4,1,4,81,128]{5,3,4,2,0,1:T(4,128)(2,1)S(1)}, u32[]{:S(2)}, u32[]{:S(2)}) %all-to-all-start) | async-done | bytes 331808 | tf_op jit(solution)/shard_map/all_to_all | solution.py:180
  219.2 3.2 %convolution_convert_fusion = bf16[128,16,1152]{2,0,1:T(8,128)(2,1)S(1)} fusion(f32[16,128,384]{2,1,0:T(8,128)S(1)} %get-tuple-element.42, f32[384]{0:T(512)S(1)} %copy-done.15, f32[128,16]{0,1:T(8,128)S(1)} %add_rsqrt_fusion.1, f32[16,384]{1,0:T(8,128)S(1)} %copy-done.9, f32[128,384]{1,0:T(8,128)S(1)} %fusion.161, bf16[384,1152]{1,0:T(8,128)(2,1)S(1)} %copy-done.14), kind=kOutput, calls=%fused_computation.42 | convolution fusion | flops 1818230784 | bytes 8979968 | tf_op jit(solution)/shard_map/tfd,de->tfe/dot_general | solution.py:57
  224.9 2.6 copy.162
  227.5 7.3 %copy.164 = bf16[128,16,8,48]{3,1,2,0:T(8,128)(2,1)} copy(bf16[128,16,8,48]{0,3,2,1:T(8,128)(2,1)} %bitcast.233) | data formatting | bytes 3145728 | tf_op jit(solution)/shard_map/reshape | solution.py:60
  237.4 7.3 %copy.165 = bf16[128,16,8,48]{3,1,2,0:T(8,128)(2,1)} copy(bf16[128,16,8,48]{0,3,2,1:T(8,128)(2,1)} %bitcast.234) | data formatting | bytes 3145728 | tf_op jit(solution)/shard_map/reshape | solution.py:61
  244.7 9.0 %fusion.162 = f32[128,8,16,16]{2,3,1,0:T(8,128)} fusion(bf16[128,16,8,48]{3,1,2,0:T(8,128)(2,1)} %copy.164, bf16[128,16,8,48]{3,1,2,0:T(8,128)(2,1)} %copy.165), kind=kOutput, calls=%fused_computation.276 | convolution fusion | flops 25165824 | bytes 4194304 | tf_op jit(solution)/shard_map/tfhe,tghe->thfg/dot_general | solution.py:63
  253.7 7.6 %copy.166 = f32[128,8,16,16]{0,3,2,1:T(8,128)} copy(f32[128,8,16,16]{2,3,1,0:T(8,128)} %fusion.162) | data formatting | bytes 2097152 | tf_op jit(solution)/shard_map/tfhe,tghe->thfg/dot_general | solution.py:63
  263.1 6.4 %copy.168 = bf16[128,8,16,16]{3,2,1,0:T(8,128)(2,1)} copy(bf16[128,8,16,16]{0,3,2,1:T(8,128)(2,1)S(1)} %divide_convert_fusion) | data formatting | bytes 1048576 | tf_op jit(solution)/shard_map/convert_element_type | solution.py:70
  271.2 7.6 %copy.167 = bf16[128,16,8,48]{3,1,2,0:T(8,128)(2,1)} copy(bf16[128,16,8,48]{0,3,2,1:T(8,128)(2,1)} %bitcast.235) | data formatting | bytes 3145728 | tf_op jit(solution)/shard_map/reshape | solution.py:62
  278.7 7.8 %convert_bitcast_fusion = bf16[128,16,8,48]{3,1,2,0:T(8,128)(2,1)} fusion(bf16[128,8,16,16]{3,2,1,0:T(8,128)(2,1)} %copy.168, bf16[128,16,8,48]{3,1,2,0:T(8,128)(2,1)} %copy.167), kind=kOutput, calls=%fused_computation.53 | convolution fusion | flops 25952256 | bytes 3670016 | tf_op jit(solution)/shard_map/thfg,tghe->tfhe/dot_general | solution.py:71
  286.5 5.5 %copy.169 = bf16[128,16,8,48]{0,3,2,1:T(8,128)(2,1)S(1)} copy(bf16[128,16,8,48]{3,1,2,0:T(8,128)(2,1)} %convert_bitcast_fusion) | data formatting | bytes 3145728 | tf_op jit(solution)/shard_map/convert_element_type | solution.py:73
  292.0 4.9 %multiply_reduce_fusion = (f32[128,16]{0,1:T(8,128)S(1)}, f32[128,16,384]{2,0,1:T(8,128)}) fusion(bf16[128,16,384]{0,2,1:T(8,128)(2,1)S(1)} %bitcast.232, bf16[384,384]{1,0:T(8,128)(2,1)S(1)} %copy-done.5, f32[16,384]{1,0:T(8,128)S(1)} %copy-done.9, f32[128,384]{1,0:T(8,128)S(1)} %fusion.161, f32[16,128,384]{2,1,0:T(8,128)} %copy-done.4), kind=kOutput, calls=%fused_computation.71 | convolution fusion | flops 607909888 | bytes 8388608 | tf_op jit(solution)/shard_map/tfd,de->tfe/dot_general | solution.py:75
  297.0 9.5 %add_convert_fusion.1 = bf16[128,16,384]{2,0,1:T(8,128)(2,1)S(1)} fusion(f32[128,16,384]{2,0,1:T(8,128)} %get-tuple-element.46, f32[384]{0:T(512)S(1)} %copy-done.16, f32[128,16]{0,1:T(8,128)S(1)} %add_rsqrt_fusion, bf16[1536,384]{1,0:T(8,128)(2,1)S(1)} %copy-done, bf16[384,1536]{1,0:T(8,128)(2,1)} %param.30), kind=kOutput, calls=%fused_computation.69 | convolution fusion | flops 4864081920 | bytes 7087616 | tf_op jit(solution)/shard_map/tfe,ed->tfd/dot_general | solution.py:83
  (195 shorter events, 63.7 us)
Async XLA Ops:
  6.5 290.4 %copy-start = (bf16[1536,384]{1,0:T(8,128)(2,1)S(1)}, bf16[1536,384]{1,0:T(8,128)(2,1)}, u32[]{:S(2)}) copy-start(bf16[1536,384]{1,0:T(8,128)(2,1)} %param.31) | copy-start | bytes 3538948
  6.5 6.8 %copy-start.1 = (s32[32,1]{0,1:T(1,128)S(1)}, s32[32,1]{0,1:T(1,128)}, u32[]{:S(2)}) copy-start(s32[32,1]{0,1:T(1,128)} %param.21) | copy-start | bytes 388
  6.5 101.1 %all-gather.2.cloned.1.call-start = ((), (), s32[]{:S(2)}) async-start(), calls=%async_computation.1 | async-start | bytes 1081344 | tf_op jit(solution)/shard_map/all_gather | solution.py:112
  7.9 26.0 %collective-permute-start = (bf16[4,1,480,128]{3,2,1,0:T(8,128)(2,1)S(1)}, bf16[4,1,480,128]{3,2,1,0:T(8,128)(2,1)S(1)}, u32[]{:S(2)}, u32[]{:S(2)}) collective-permute-start(bf16[4,1,480,128]{3,2,1,0:T(8,128)(2,1)S(1)} %get-tuple-element.39), channel_id=1, source_target_pairs={{0,1},{1,2},{2,3},{3,4},{4,5},{5,6},{6,7},{8,9},{9,10},{10,11},{11... | collective-permute-start | bytes 1474568 | tf_op jit(solution)/shard_map/ppermute | solution.py:19
  10.3 23.5 %collective-permute-start.1 = (bf16[4,1,480,128]{3,2,1,0:T(8,128)(2,1)S(1)}, bf16[4,1,480,128]{3,2,1,0:T(8,128)(2,1)S(1)}, u32[]{:S(2)}, u32[]{:S(2)}) collective-permute-start(bf16[4,1,480,128]{3,2,1,0:T(8,128)(2,1)S(1)} %get-tuple-element.40), channel_id=1, source_target_pairs={{1,0},{2,1},{3,2},{4,3},{5,4},{6,5},{7,6},{9,8},{10,9},{11,10},{12... | collective-permute-start | bytes 1474568 | tf_op jit(solution)/shard_map/ppermute | solution.py:21
  23.1 4.2 %copy-start.6 = (bf16[3,3,128,128]{3,2,1,0:T(8,128)(2,1)S(1)}, bf16[3,3,128,128]{3,2,1,0:T(8,128)(2,1)}, u32[]{:S(2)}) copy-start(bf16[3,3,128,128]{3,2,1,0:T(8,128)(2,1)} %param.17) | copy-start | bytes 884740
  27.2 6.6 %copy-start.3 = (bf16[4,8,480,128]{3,2,1,0:T(8,128)(2,1)S(1)}, bf16[4,8,480,128]{3,2,1,0:T(8,128)(2,1)}, u32[]{:S(2)}) copy-start(bf16[4,8,480,128]{3,2,1,0:T(8,128)(2,1)} %param.16) | copy-start | bytes 11796484
  37.5 17.6 %copy-start.2 = (bf16[4,10,482,128]{3,2,1,0:T(8,128)(2,1)}, bf16[4,10,482,128]{3,2,1,0:T(8,128)(2,1)S(1)}, u32[]{:S(2)}) copy-start(bf16[4,10,482,128]{3,2,1,0:T(8,128)(2,1)S(1)} %fusion.14) | copy-start | bytes 14807044
  95.8 9.1 %copy-start.11 = (s32[4,32]{1,0:T(4,128)S(1)}, s32[4,32]{1,0:T(4,128)}, u32[]{:S(2)}) copy-start(s32[4,32]{1,0:T(4,128)} %param.19) | copy-start | bytes 1540
  95.8 9.9 %copy-start.12 = (s32[4,32]{1,0:T(4,128)S(1)}, s32[4,32]{1,0:T(4,128)}, u32[]{:S(2)}) copy-start(s32[4,32]{1,0:T(4,128)} %param.20) | copy-start | bytes 1540
  95.8 14.4 %collective-permute-start.2 = (bf16[4,4,480,128]{3,2,1,0:T(8,128)(2,1)}, bf16[4,4,480,128]{3,2,1,0:T(8,128)(2,1)S(1)}, u32[]{:S(2)}, u32[]{:S(2)}) collective-permute-start(bf16[4,4,480,128]{3,2,1,0:T(8,128)(2,1)} %get-tuple-element.37), channel_id=1, source_target_pairs={{0,1},{1,2},{2,3},{3,4},{4,5},{5,6},{6,7},{8,9},{9,10},{10,11},{11... | collective-permute-start | bytes 5898248 | tf_op jit(solution)/shard_map/ppermute | solution.py:19
  101.2 9.0 %collective-permute-start.3 = (bf16[4,4,480,128]{3,2,1,0:T(8,128)(2,1)}, bf16[4,4,480,128]{3,2,1,0:T(8,128)(2,1)}, u32[]{:S(2)}, u32[]{:S(2)}) collective-permute-start(bf16[4,4,480,128]{3,2,1,0:T(8,128)(2,1)} %get-tuple-element.38), channel_id=1, source_target_pairs={{1,0},{2,1},{3,2},{4,3},{5,4},{6,5},{7,6},{9,8},{10,9},{11,10},{12... | collective-permute-start | bytes 5898248 | tf_op jit(solution)/shard_map/ppermute | solution.py:21
  139.7 21.3 %collective-permute-start.4 = (bf16[12,4,81,128]{3,1,2,0:T(4,128)(2,1)}, bf16[12,4,81,128]{3,1,2,0:T(4,128)(2,1)S(1)}, u32[]{:S(2)}, u32[]{:S(2)}) collective-permute-start(bf16[12,4,81,128]{3,1,2,0:T(4,128)(2,1)} %copy.142), channel_id=1, source_target_pairs={{0,1},{1,0},{2,3},{3,2},{4,5},{5,4},{6,7},{7,6},{8,9},{9,8},{10,11... | collective-permute-start | bytes 2985992 | tf_op jit(solution)/shard_map/ppermute | solution.py:31
  166.3 17.3 %collective-permute-start.5 = (bf16[8,4,81,128]{3,0,2,1:T(8,128)(2,1)S(1)}, bf16[8,4,81,128]{3,0,2,1:T(8,128)(2,1)S(1)}, u32[]{:S(2)}, u32[]{:S(2)}) collective-permute-start(bf16[8,4,81,128]{3,0,2,1:T(8,128)(2,1)S(1)} %copy.151), channel_id=1, source_target_pairs={{0,2},{1,3},{2,0},{3,1},{4,6},{5,7},{6,4},{7,5},{8,10},{9,11},{10,... | collective-permute-start | bytes 1990664 | tf_op jit(solution)/shard_map/ppermute | solution.py:31
  185.2 27.5 %copy-start.13 = (s32[128]{0:T(128)S(1)}, s32[128]{0:T(128)}, u32[]{:S(2)}) copy-start(s32[128]{0:T(128)} %param.22) | copy-start | bytes 1540
  185.2 27.5 %copy-start.7 = (bf16[128,128]{1,0:T(8,128)(2,1)S(1)}, bf16[128,128]{1,0:T(8,128)(2,1)}, u32[]{:S(2)}) copy-start(bf16[128,128]{1,0:T(8,128)(2,1)} %param.18) | copy-start | bytes 98308
  185.2 27.5 %copy-start.8 = (bf16[128,384]{1,0:T(8,128)(2,1)S(1)}, bf16[128,384]{1,0:T(8,128)(2,1)}, u32[]{:S(2)}) copy-start(bf16[128,384]{1,0:T(8,128)(2,1)} %param.24) | copy-start | bytes 294916
  185.2 33.1 %copy-start.9 = (f32[16,384]{1,0:T(8,128)S(1)}, f32[16,384]{1,0:T(8,128)}, u32[]{:S(2)}) copy-start(f32[16,384]{1,0:T(8,128)} %param.25) | copy-start | bytes 73732
  185.2 33.1 %copy-start.10 = (bf16[81,384]{1,0:T(8,128)(2,1)S(1)}, bf16[81,384]{1,0:T(8,128)(2,1)}, u32[]{:S(2)}) copy-start(bf16[81,384]{1,0:T(8,128)(2,1)} %param.23) | copy-start | bytes 186628
  188.2 18.5 %collective-permute-start.6 = (bf16[4,4,81,128]{3,2,1,0:T(8,128)(2,1)S(1)}, bf16[4,4,81,128]{3,2,1,0:T(8,128)(2,1)S(1)}, u32[]{:S(2)}, u32[]{:S(2)}) collective-permute-start(bf16[4,4,81,128]{3,2,1,0:T(8,128)(2,1)S(1)} %gather_fusion.10), channel_id=1, source_target_pairs={{0,4},{1,5},{2,6},{3,7},{4,0},{5,1},{6,2},{7,3},{8,12},{9,13},{10,... | collective-permute-start | bytes 995336 | tf_op jit(solution)/shard_map/ppermute | solution.py:31
  206.8 12.4 %copy-start.15 = (f32[384]{0:T(512)S(1)}, f32[384]{0:T(512)}, u32[]{:S(2)}) copy-start(f32[384]{0:T(512)} %param.26) | copy-start | bytes 4612
  207.4 11.7 %copy-start.14 = (bf16[384,1152]{1,0:T(8,128)(2,1)S(1)}, bf16[384,1152]{1,0:T(8,128)(2,1)}, u32[]{:S(2)}) copy-start(bf16[384,1152]{1,0:T(8,128)(2,1)} %param.27) | copy-start | bytes 2654212
  208.9 9.3 %all-to-all-start = ((bf16[1,4,1,4,81,128]{5,3,4,2,0,1:T(4,128)(2,1)}), bf16[1,4,1,4,81,128]{5,3,4,2,0,1:T(4,128)(2,1)S(1)}, u32[]{:S(2)}, u32[]{:S(2)}) async-start(bf16[1,4,1,4,81,128]{5,3,4,2,0,1:T(4,128)(2,1)} %copy.159), calls=%async_computation | async-start | bytes 663552 | tf_op jit(solution)/shard_map/all_to_all | solution.py:180
  219.1 3.2 %copy-start.4 = (f32[16,128,384]{2,1,0:T(8,128)}, f32[16,128,384]{2,1,0:T(8,128)S(1)}, u32[]{:S(2)}) copy-start(f32[16,128,384]{2,1,0:T(8,128)S(1)} %get-tuple-element.42) | copy-start | bytes 9437188
  286.5 5.5 %copy-start.5 = (bf16[384,384]{1,0:T(8,128)(2,1)S(1)}, bf16[384,384]{1,0:T(8,128)(2,1)}, u32[]{:S(2)}) copy-start(bf16[384,384]{1,0:T(8,128)(2,1)} %param.28) | copy-start | bytes 884740
  292.0 5.0 %copy-start.16 = (f32[384]{0:T(512)S(1)}, f32[384]{0:T(512)}, u32[]{:S(2)}) copy-start(f32[384]{0:T(512)} %param.29) | copy-start | bytes 4612
Sparse Core Ops, SparseCore 0:
  11.8 58.4 all-gather.1
where the time goes:
time: 321 us; the launch traced here: 316 us
  local copies, waits for them, and re-layouts  107 us (33%)
  matrix products  97.7 us (30%)
  waiting for transfers between devices  37.2 us (12%)
  starting transfers between devices  37.1 us (12%)
  other arithmetic  22.6 us (7%)
  between operations  14.5 us (5%)
    dot_general x9, matrix products, convolve(): jnp.einsum('fhwc,cd->fhwd', wide[:, a:a + out_rows, b:b + cols], w_conv[a...  60.6 us
    ppermute x3, waiting for transfers between devices, from_partner(): return lax.ppermute(value, axis, pairs)  31.8 us
    ppermute x3, starting transfers between devices, from_partner(): return lax.ppermute(value, axis, pairs)  23 us
    concatenate x1, local copies, waits for them, and re-layouts, extended_2(): jnp.concatenate([lax.ppermute(tail, axis, [(i, (i + 1) % count) for i in...  12.5 us
    concatenate x2, other arithmetic, extended_2(): jnp.concatenate([lax.ppermute(tail, axis, [(i, (i + 1) % count) for i in...  10.1 us
    dot_general x1, matrix products, token_layer(): jnp.einsum('tfe,ed->tfd', hidden, w_down, preferred_element_type=jnp.floa...  9.54 us
    dot_general x1, matrix products, token_layer(): jnp.einsum('tfhe,tghe->thfg', query, keys, preferred_element_type=jnp.flo...  9.01 us
    ppermute x2, starting transfers between devices, extended_2(): lax.ppermute(tail, axis, [(i, (i + 1) % count) for i in range(ends)])  7.78 us
  transfers between devices with their start and end apart: 9, of which 4 were waited for; matrix products, arithmetic and copies ran while one was open for 30% of the time, Pallas kernels for 0%

commit v1 on v0

v1 whole, which is shorter than its diff:
```python
import functools

import jax
import jax.numpy as jnp
from jax import lax
from jax.experimental import pallas as pl
from jax.experimental.pallas import tpu as pltpu
from jax.sharding import PartitionSpec as P

HEADS = 8
WIN = 9
QBLK = 128
CELLS = 96
REACH = WIN // 2
GROUP = 8
F32 = jnp.float32
BF16 = jnp.bfloat16
MESH = pl.DeviceIdType.MESH


def reversed_bits(value, bits):
    out = value * 0
    for bit in range(bits):
        out = out + ((value // 2**bit) % 2) * 2 ** (bits - 1 - bit)
    return out


def window_kernel(n_tiles, n_frames, owners, row_off, col_off, feat, w_cat, out, padded, conv, win):
    frame = pl.program_id(0)
    tile = lax.axis_index("tiles")
    rows, cols, chans = feat.shape[1:]
    blocks = owners.shape[0]
    per_group = blocks // n_frames
    blk_dev = per_group // n_tiles
    bits = n_tiles.bit_length() - 1

    @pl.when(frame == 0)
    def _():
        blank = jnp.zeros((2, cols, chans), BF16)
        padded[0:2] = blank
        padded[rows + 2 : rows + 4] = blank
        win[...] = jnp.zeros_like(win)
        conv[:, cols:] = jnp.zeros((rows + 2, 16, chans), F32)

    padded[2 : rows + 2] = feat[0]

    def conv_row(y, carry):
        wide = jnp.concatenate([padded[y], padded[y + 1], padded[y + 2]], axis=-1)
        parts = jnp.dot(wide, w_cat[...], preferred_element_type=F32)
        edge = jnp.zeros((1, chans), F32)
        left = jnp.concatenate([edge, parts[: cols - 1, :chans]], axis=0)
        right = jnp.concatenate([parts[1:, 2 * chans :], edge], axis=0)
        conv[y, :cols] = left + parts[:, chans : 2 * chans] + right
        return carry

    lax.fori_loop(0, rows + 2, conv_row, 0)

    def cut(block, carry):
        within = block % per_group
        slot = reversed_bits(within // blk_dev, bits)
        place = (block // per_group) * blk_dev + within % blk_dev
        owner = owners[block]
        first = owner * rows + row_off[frame, block] - REACH
        local = first - tile * rows
        touches = (local <= rows) & (local + WIN - 1 >= -1)

        @pl.when(touches)
        def _():
            col = col_off[frame, block]
            for i in range(WIN):
                row = local + i
                there = (row >= -1) & (row <= rows)
                there = there & (first + i >= 0) & (first + i < n_tiles * rows)
                cells = conv[jnp.clip(row + 1, 0, rows + 1), pl.ds(col, WIN), :]
                win[i * WIN : (i + 1) * WIN, :] = jnp.where(there, cells, 0.0)
            out[0, slot, place] = win[...].astype(BF16)

        @pl.when(jnp.logical_not(touches))
        def _():
            out[0, slot, place] = jnp.zeros((CELLS, chans), BF16)

        return carry

    lax.fori_loop(0, blocks, cut, 0)


def exchange_kernel(n_tiles, n_frames, parts, out, *scratch):
    levels = n_tiles.bit_length() - 1
    sums, lands = scratch[:levels], scratch[levels : 2 * levels]
    send_sem, recv_sem, out_send, out_recv = scratch[2 * levels :]
    tile, group = lax.axis_index("tiles"), lax.axis_index("frames")
    frame_dev = parts.shape[0]
    blk_dev = out.shape[1]

    partners = []
    for level in range(levels):
        bit = (tile // 2**level) % 2
        partners.append((group, tile + (1 - 2 * bit) * 2**level))
    peers = [((group + step) % n_frames, tile) for step in range(1, n_frames)]
    barrier = pltpu.get_barrier_semaphore()
    for device in partners + peers:
        pl.semaphore_signal(barrier, inc=1, device_id=device, device_id_type=MESH)
    pl.semaphore_wait(barrier, len(partners) + len(peers))

    def halving(level, frame):
        source = parts if level == 0 else sums[level - 1]
        count = n_tiles >> (level + 1)
        bit = (tile // 2**level) % 2
        copy = pltpu.make_async_remote_copy(
            src_ref=source.at[frame, pl.ds((1 - bit) * count, count)],
            dst_ref=lands[level].at[frame],
            send_sem=send_sem.at[level, frame],
            recv_sem=recv_sem.at[level, frame],
            device_id=partners[level],
            device_id_type=MESH,
        )
        return copy, source, bit * count, count

    pending = []
    for frame in range(frame_dev):
        halving(0, frame)[0].start()
    for level in range(levels):
        for frame in range(frame_dev):
            copy, source, start, count = halving(level, frame)
            copy.wait_recv()
            pending.append(copy)

            def add(i, carry):
                both = source[frame, start + i].astype(F32) + lands[level][frame, i].astype(F32)
                sums[level][frame, i] = both.astype(BF16)
                return carry

            lax.fori_loop(0, count, add, 0)
            if level + 1 < levels:
                halving(level + 1, frame)[0].start()
            else:
                for step, peer in enumerate(peers):
                    away = pltpu.make_async_remote_copy(
                        src_ref=sums[level].at[frame, 0, pl.ds(peer[0] * blk_dev, blk_dev)],
                        dst_ref=out.at[group * frame_dev + frame],
                        send_sem=out_send.at[step, frame],
                        recv_sem=out_recv.at[step, frame],
                        device_id=peer,
                        device_id_type=MESH,
                    )
                    away.start()
                out[group * frame_dev + frame] = sums[level][frame, 0, pl.ds(group * blk_dev, blk_dev)]
    for copy in pending:
        copy.wait_send()
    for step, peer in enumerate(peers):
        for frame in range(frame_dev):
            giver = (group + n_frames - step - 1) % n_frames
            pltpu.make_async_remote_copy(
                src_ref=sums[levels - 1].at[frame, 0, pl.ds(peer[0] * blk_dev, blk_dev)],
                dst_ref=out.at[giver * frame_dev + frame],
                send_sem=out_send.at[step, frame],
                recv_sem=out_recv.at[step, frame],
                device_id=peer,
                device_id_type=MESH,
            ).wait()


def rms_scale(values, gain):
    return values * lax.rsqrt(jnp.mean(values * values, axis=-1, keepdims=True) + 1e-06) * gain


def token_kernel(
    bundle, patch, query, starts, w_corr, w_feat, time_embed, gain_attn, w_qkv_t, w_attn_out, gain_mlp,
    w_up, w_down, out, tokens,
):
    step = pl.program_id(0)
    frames = patch.shape[0]
    chans = query.shape[1]
    width = w_feat.shape[1]
    head = width // HEADS
    span = GROUP * frames
    per_block = QBLK // (GROUP * bundle)

    @pl.when(step % per_block == 0)
    def _():
        queries = query[...]
        feat = jnp.dot(queries, w_feat[...], preferred_element_type=F32)
        for frame in range(frames):
            corr = lax.dot_general(
                patch[frame, 0], queries, (((1,), (1,)), ((), ())), preferred_element_type=F32
            ) * chans ** (-0.5)
            part = lax.dot_general(
                corr.astype(BF16), w_corr[...], (((0,), (0,)), ((), ())), preferred_element_type=F32
            )
            tokens[frame] = part + feat + time_embed[frame : frame + 1, :]

    first = (step % per_block) * (GROUP * bundle)
    x = jnp.concatenate(
        [
            tokens[:, pl.ds(pl.multiple_of(first + GROUP * g, GROUP), GROUP), :].reshape(span, width)
            for g in range(bundle)
        ],
        axis=0,
    )
    normed = rms_scale(x, gain_attn[...]).astype(BF16)
    qkv = lax.dot_general(
        w_qkv_t[...], normed, (((1,), (1,)), ((), ())), preferred_element_type=F32
    ).astype(BF16)
    key_at = lax.broadcasted_iota(jnp.int32, (span, span), 0)
    query_at = lax.broadcasted_iota(jnp.int32, (span, span), 1)
    same = (key_at % GROUP) == (query_at % GROUP)
    gathered = []
    for g in range(bundle):
        at = slice(g * span, (g + 1) * span)
        valid = same & ((key_at // GROUP) >= starts[0, g : g + 1, :])
        heads = []
        for h in range(HEADS):
            query_h = qkv[h * head : (h + 1) * head, at]
            key_h = qkv[width + h * head : width + (h + 1) * head, at]
            value_h = qkv[2 * width + h * head : 2 * width + (h + 1) * head, at]
            scores = lax.dot_general(
                key_h, query_h, (((0,), (0,)), ((), ())), preferred_element_type=F32
            ) * head ** (-0.5)
            scores = jnp.where(valid, scores, -1e30)
            weights = jnp.exp(scores - jnp.max(scores, axis=0, keepdims=True))
            total = jnp.sum(weights, axis=0, keepdims=True)
            mixed_h = jnp.dot(value_h, weights.astype(BF16), preferred_element_type=F32)
            heads.append((mixed_h / total).astype(BF16))
        gathered.append(jnp.concatenate(heads, axis=0))
    attended = jnp.concatenate(gathered, axis=1)
    mixed = x + lax.dot_general(
        attended, w_attn_out[...], (((0,), (0,)), ((), ())), preferred_element_type=F32
    )
    normed2 = rms_scale(mixed, gain_mlp[...]).astype(BF16)
    hidden = jax.nn.gelu(
        jnp.dot(normed2, w_up[...], preferred_element_type=F32), approximate=True
    ).astype(BF16)
    result = mixed + jnp.dot(hidden, w_down[...], preferred_element_type=F32)
    result = result.astype(BF16)
    move = (query_at == (key_at % frames) * GROUP + key_at // frames).astype(BF16)
    for g in range(bundle):
        at = slice(g * span, (g + 1) * span)
        out[at, :] = jnp.dot(move, result[at, :], preferred_element_type=F32).astype(BF16)


def body(
    features, w_conv, query_feats, offset_rows, offset_cols, owners, start_frames, w_corr, w_feat,
    time_embed, gain_attn, w_qkv, w_attn_out, gain_mlp, w_up, w_down,
):
    n_tiles = lax.axis_size("tiles")
    n_frames = lax.axis_size("frames")
    frame_dev, rows, cols, chans = features.shape
    blocks = owners.shape[0]
    blk_dev = blocks // (n_frames * n_tiles)
    lots = n_frames * blk_dev
    levels = n_tiles.bit_length() - 1
    frames_total = frame_dev * n_frames
    width = w_feat.shape[1]
    whole = pl.BlockSpec(memory_space=pltpu.VMEM)
    scalars = pl.BlockSpec(memory_space=pltpu.SMEM)

    w_cat = w_conv.transpose(0, 2, 1, 3).reshape(3 * chans, 3 * chans)
    parts = pl.pallas_call(
        functools.partial(window_kernel, n_tiles, n_frames),
        grid=(frame_dev,),
        out_shape=jax.ShapeDtypeStruct((frame_dev, n_tiles, lots, CELLS, chans), BF16),
        in_specs=[
            scalars,
            scalars,
            scalars,
            pl.BlockSpec((1, rows, cols, chans), lambda f: (f, 0, 0, 0)),
            pl.BlockSpec((3 * chans, 3 * chans), lambda f: (0, 0)),
        ],
        out_specs=pl.BlockSpec((1, n_tiles, lots, CELLS, chans), lambda f: (f, 0, 0, 0, 0)),
        scratch_shapes=[
            pltpu.VMEM((rows + 4, cols, chans), BF16),
            pltpu.VMEM((rows + 2, cols + 16, chans), F32),
            pltpu.VMEM((CELLS, chans), F32),
        ],
    )(owners[:, 0], offset_rows, offset_cols, features, w_cat)

    halves = [
        pltpu.VMEM((frame_dev, n_tiles >> (level + 1), lots, CELLS, chans), BF16)
        for level in range(levels)
    ]
    patch = pl.pallas_call(
        functools.partial(exchange_kernel, n_tiles, n_frames),
        out_shape=jax.ShapeDtypeStruct((frames_total, blk_dev, CELLS, chans), BF16),
        in_specs=[whole],
        out_specs=whole,
        scratch_shapes=halves
        + halves
        + [pltpu.SemaphoreType.DMA((levels, frame_dev))] * 2
        + [pltpu.SemaphoreType.DMA((n_frames - 1, frame_dev))] * 2,
        compiler_params=pltpu.CompilerParams(collective_id=0, has_side_effects=True),
    )(parts)

    bundle = 4
    span = GROUP * frames_total
    tracks = blk_dev * QBLK
    per_block = QBLK // (GROUP * bundle)
    starts = jnp.tile(start_frames.reshape(-1, bundle, GROUP), (1, 1, frames_total))
    w_corr_pad = jnp.pad(w_corr, ((0, CELLS - WIN * WIN), (0, 0)))

    def fixed(shape):
        return pl.BlockSpec(shape, lambda s: (0,) * len(shape))

    refined = pl.pallas_call(
        functools.partial(token_kernel, bundle),
        grid=(tracks // (GROUP * bundle),),
        out_shape=jax.ShapeDtypeStruct((tracks * frames_total, width), BF16),
        in_specs=[
            pl.BlockSpec((frames_total, 1, CELLS, chans), lambda s: (0, s // per_block, 0, 0)),
            pl.BlockSpec((QBLK, chans), lambda s: (s // per_block, 0)),
            pl.BlockSpec((1, bundle, span), lambda s: (s, 0, 0)),
            fixed((CELLS, width)),
            fixed(w_feat.shape),
            fixed(time_embed.shape),
            fixed((1, width)),
            fixed((3 * width, width)),
            fixed(w_attn_out.shape),
            fixed((1, width)),
            fixed(w_up.shape),
            fixed(w_down.shape),
        ],
        out_specs=pl.BlockSpec((bundle * span, width), lambda s: (s, 0)),
        scratch_shapes=[pltpu.VMEM((frames_total, QBLK, width), F32)],
    )(
        patch, query_feats, starts, w_corr_pad, w_feat, time_embed, gain_attn[None], w_qkv.T,
        w_attn_out, gain_mlp[None], w_up, w_down,
    )
    return refined.reshape(tracks, frames_total, width)


def solution(mesh):
    placed = (
        P("frames", "tiles", None, None),
        P(),
        P(("frames", "tiles"), None),
        P("frames", None),
        P("frames", None),
        P(),
        P(("frames", "tiles")),
    ) + (P(),) * 9
    return jax.shard_map(
        body,
        mesh=mesh,
        in_specs=placed,
        out_specs=P(("frames", "tiles"), None, None),
        check_vma=False,
    )
```

time: 321 us -> 117 us (0.36); the launches traced: 316 us -> 117 us
  Pallas kernels: 0 us -> 111 us
  local copies, waits for them, and re-layouts: 107 us -> 5.96 us
  matrix products: 97.7 us -> 0 us
  waiting for transfers between devices: 37.2 us -> 0 us
  starting transfers between devices: 37.1 us -> 0 us
  other arithmetic: 22.6 us -> 0 us
  between operations: 14.5 us -> 0.07 us
    pallas_call x0 -> x3, Pallas kernels: none -> 111 us  [the longest x1 42.7 us: body(): pl.pallas_call(functools.partial(token_kernel, bundle), grid=(tracks // (...]
    dot_general x17 -> x0, matrix products: 97.7 us -> none  [the longest x9 60.6 us: convolve(): jnp.einsum('fhwc,cd->fhwd', wide[:, a:a + out_rows, b:b + cols], w_conv[a...]
    ppermute x7 -> x0, starting transfers between devices: 33.3 us -> none  [the longest x3 23 us: from_partner(): return lax.ppermute(value, axis, pairs)]
    gather x42 -> x0, local copies, waits for them, and re-layouts: 32.4 us -> none  [the longest x5 7.04 us: frame_patch(): lax.dynamic_slice(frame, (row, col, zero_start), (WIN, WIN, chans))]
    ppermute x7 -> x0, waiting for transfers between devices: 31.8 us -> none  [the longest x3 31.8 us: from_partner(): return lax.ppermute(value, axis, pairs)]
    reshape x4 -> x0, local copies, waits for them, and re-layouts: 23 us -> none  [the longest x1 7.55 us: token_layer(): values = qkv[..., 2 * width:].reshape(tracks, frames, HEADS, head)]
    slice x8 -> x0, local copies, waits for them, and re-layouts: 15 us -> none  [the longest x2 5.67 us: extended_2(): lax.slice_in_dim(cells, cells.shape[dim] - width, cells.shape[dim], axis=...]
    convert_element_type x3 -> x0, local copies, waits for them, and re-layouts: 14 us -> none  [the longest x1 6.45 us: token_layer(): (weights / jnp.sum(weights, axis=-1, keepdims=True)).astype(jnp.bfloat16)]
  transfers between devices with their start and end apart: 9 -> 0, of which waited for: 4 -> 0; matrix products, arithmetic and copies ran while one was open for 30% -> 0% of each run, Pallas kernels for 0% -> 0%
where the time goes in v1:
time: 117 us
  Pallas kernels  111 us (95%)
  local copies, waits for them, and re-layouts  5.96 us (5%)
    pallas_call x1, Pallas kernels, body(): pl.pallas_call(functools.partial(token_kernel, bundle), grid=(tracks // (...  42.7 us
    pallas_call x1, Pallas kernels, body(): pl.pallas_call(functools.partial(exchange_kernel, n_tiles, n_frames), out...  41.9 us
    pallas_call x1, Pallas kernels, body(): pl.pallas_call(functools.partial(window_kernel, n_tiles, n_frames), grid=...  26.5 us

profile of v1, /device:TPU:0, one launch (start us, length us, event | category | flops | bytes accessed | tf_op | source)
XLA Modules:
  0.0 117.1 jit_solution(17903021115443454210)
XLA Ops:
  0.0 1.2 %copy.19 = bf16[3,128,3,128]{3,2,1,0:T(4,128)(2,1)S(1)} copy(bf16[3,128,3,128]{3,1,2,0:T(8,128)(2,1)} %bitcast.14) | data formatting | bytes 589824 | tf_op jit(solution)/shard_map/transpose | solution.py:257
  1.2 0.8 copy.23
  2.0 26.5 %shard_map.154.parts = bf16[4,8,4,96,128]{4,3,2,1,0:T(8,128)(2,1)} custom-call(s32[32]{0:T(128)} %bitcast.15, s32[4,32]{1,0:T(4,128)} %row_off.1, s32[4,32]{1,0:T(4,128)} %col_off.1, bf16[4,8,480,128]{3,2,1,0:T(8,128)(2,1)} %feat.1, bf16[384,384]{1,0:T(8,128)(2,1)} %bitcast.13), custom_call_target="tpu_custom_call" | custom-call | tf_op jit(solution)/shard_map/pallas_call | solution.py:258
  28.5 0.0 copy-start
  28.5 41.9 %shard_map.155.patch = bf16[16,1,96,128]{3,2,1,0:T(8,128)(2,1)} custom-call(bf16[4,8,4,96,128]{4,3,2,1,0:T(8,128)(2,1)} %shard_map.154.parts), custom_call_target="tpu_custom_call" | custom-call | tf_op jit(solution)/shard_map/pallas_call | solution.py:281
  70.4 0.0 copy-done
  70.4 0.0 copy-start.4
  70.4 0.0 copy-start.1
  70.4 0.0 copy-start.2
  70.4 0.0 copy-start.3
  70.5 1.3 %copy.20 = bf16[384,1152]{0,1:T(8,128)(2,1)} copy(bf16[384,1152]{1,0:T(8,128)(2,1)S(1)} %copy-done) | data formatting | bytes 1769472 | tf_op args[11]
  71.8 0.0 copy-done.4
  71.8 0.1 tile.10
  71.9 0.7 tile.12.starts
  72.6 0.0 copy-done.1
  72.6 0.7 pad.4.w_corr
  73.3 0.0 copy-done.2
  73.3 0.6 broadcast_in_dim.6.gain_attn
  73.9 0.0 copy-done.3
  73.9 0.6 broadcast_in_dim.7.gain_mlp
  74.4 42.7 %shard_map.156 = bf16[2048,384]{1,0:T(8,128)(2,1)} custom-call(bf16[16,1,96,128]{3,2,1,0:T(8,128)(2,1)} %shard_map.155.patch, bf16[128,128]{1,0:T(8,128)(2,1)} %query.1, s32[4,4,128]{2,1,0:T(4,128)} %tile.12.starts, bf16[96,384]{1,0:T(8,128)(2,1)} %pad.4.w_corr, bf16[128,384]{1,0:T(8,128)(2,1)} %w_feat.1, f32[16,384]{1,0:T(8,128)} %time_embed.1, ...), custom_call_target="tpu_custom_call" | custom-call | tf_op jit(solution)/shard_map/pallas_call | solution.py:303
  (1 shorter events, 0.0 us)
Async XLA Ops:
  28.5 41.9 %copy-start = (bf16[384,1152]{1,0:T(8,128)(2,1)S(1)}, bf16[384,1152]{1,0:T(8,128)(2,1)}, u32[]{:S(2)}) copy-start(bf16[384,1152]{1,0:T(8,128)(2,1)} %param.27) | copy-start | bytes 2654212
  70.4 1.4 %copy-start.4 = (s32[128]{0:T(128)S(1)}, s32[128]{0:T(128)}, u32[]{:S(2)}) copy-start(s32[128]{0:T(128)} %param.22) | copy-start | bytes 1540
  70.4 2.2 %copy-start.1 = (bf16[81,384]{1,0:T(8,128)(2,1)S(1)}, bf16[81,384]{1,0:T(8,128)(2,1)}, u32[]{:S(2)}) copy-start(bf16[81,384]{1,0:T(8,128)(2,1)} %param.23) | copy-start | bytes 186628
  70.4 2.8 %copy-start.2 = (f32[384]{0:T(512)S(1)}, f32[384]{0:T(512)}, u32[]{:S(2)}) copy-start(f32[384]{0:T(512)} %param.26) | copy-start | bytes 4612
  70.4 3.4 %copy-start.3 = (f32[384]{0:T(512)S(1)}, f32[384]{0:T(512)}, u32[]{:S(2)}) copy-start(f32[384]{0:T(512)} %param.29) | copy-start | bytes 4612

commit v2 on v1

--- a/solution.py
+++ b/solution.py
@@ -25,73 +25,23 @@
     return out
 
 
-def window_kernel(n_tiles, n_frames, owners, row_off, col_off, feat, w_cat, out, padded, conv, win):
-    frame = pl.program_id(0)
-    tile = lax.axis_index("tiles")
-    rows, cols, chans = feat.shape[1:]
+def window_kernel(
+    n_tiles, n_frames, owners, row_off, col_off, feat, w_conv, out, w_cat, padded, conv, win, parts, *scratch
+):
+    levels = n_tiles.bit_length() - 1
+    sums, lands = scratch[:levels], scratch[levels : 2 * levels]
+    feat_sem, send_sem, recv_sem, out_send, out_recv = scratch[2 * levels :]
+    tile, group = lax.axis_index("tiles"), lax.axis_index("frames")
+    frame_dev, rows, cols, chans = feat.shape
     blocks = owners.shape[0]
     per_group = blocks // n_frames
-    blk_dev = per_group // n_tiles
-    bits = n_tiles.bit_length() - 1
-
-    @pl.when(frame == 0)
-    def _():
-        blank = jnp.zeros((2, cols, chans), BF16)
-        padded[0:2] = blank
-        padded[rows + 2 : rows + 4] = blank
-        win[...] = jnp.zeros_like(win)
-        conv[:, cols:] = jnp.zeros((rows + 2, 16, chans), F32)
-
-    padded[2 : rows + 2] = feat[0]
-
-    def conv_row(y, carry):
-        wide = jnp.concatenate([padded[y], padded[y + 1], padded[y + 2]], axis=-1)
-        parts = jnp.dot(wide, w_cat[...], preferred_element_type=F32)
-        edge = jnp.zeros((1, chans), F32)
-        left = jnp.concatenate([edge, parts[: cols - 1, :chans]], axis=0)
-        right = jnp.concatenate([parts[1:, 2 * chans :], edge], axis=0)
-        conv[y, :cols] = left + parts[:, chans : 2 * chans] + right
-        return carry
-
-    lax.fori_loop(0, rows + 2, conv_row, 0)
-
-    def cut(block, carry):
-        within = block % per_group
-        slot = reversed_bits(within // blk_dev, bits)
-        place = (block // per_group) * blk_dev + within % blk_dev
-        owner = owners[block]
-        first = owner * rows + row_off[frame, block] - REACH
-        local = first - tile * rows
-        touches = (local <= rows) & (local + WIN - 1 >= -1)
-
-        @pl.when(touches)
-        def _():
-            col = col_off[frame, block]
-            for i in range(WIN):
-                row = local + i
-                there = (row >= -1) & (row <= rows)
-                there = there & (first + i >= 0) & (first + i < n_tiles * rows)
-                cells = conv[jnp.clip(row + 1, 0, rows + 1), pl.ds(col, WIN), :]
-                win[i * WIN : (i + 1) * WIN, :] = jnp.where(there, cells, 0.0)
-            out[0, slot, place] = win[...].astype(BF16)
-
-        @pl.when(jnp.logical_not(touches))
-        def _():
-            out[0, slot, place] = jnp.zeros((CELLS, chans), BF16)
-
-        return carry
-
-    lax.fori_loop(0, blocks, cut, 0)
-
-
-def exchange_kernel(n_tiles, n_frames, parts, out, *scratch):
-    levels = n_tiles.bit_length() - 1
-    sums, lands = scratch[:levels], scratch[levels : 2 * levels]
-    send_sem, recv_sem, out_send, out_recv = scratch[2 * levels :]
-    tile, group = lax.axis_index("tiles"), lax.axis_index("frames")
-    frame_dev = parts.shape[0]
     blk_dev = out.shape[1]
 
+    def fetch(frame):
+        return pltpu.make_async_copy(feat.at[frame], padded.at[frame, pl.ds(2, rows)], feat_sem.at[frame])
+
+    for frame in range(frame_dev):
+        fetch(frame).start()
     partners = []
     for level in range(levels):
         bit = (tile // 2**level) % 2
@@ -100,7 +50,17 @@
     barrier = pltpu.get_barrier_semaphore()
     for device in partners + peers:
         pl.semaphore_signal(barrier, inc=1, device_id=device, device_id_type=MESH)
-    pl.semaphore_wait(barrier, len(partners) + len(peers))
+
+    blank = jnp.zeros((2, cols, chans), BF16)
+    for frame in range(frame_dev):
+        padded[frame, 0:2] = blank
+        padded[frame, rows + 2 : rows + 4] = blank
+    win[...] = jnp.zeros_like(win)
+    conv[rows + 2] = jnp.zeros(conv.shape[1:], F32)
+    conv[:, cols:] = jnp.zeros((rows + 3, conv.shape[1] - cols, chans), F32)
+    for a in range(3):
+        for b in range(3):
+            w_cat[a * chans : (a + 1) * chans, b * chans : (b + 1) * chans] = w_conv[a, b]
 
     def halving(level, frame):
         source = parts if level == 0 else sums[level - 1]
@@ -116,48 +76,91 @@
         )
         return copy, source, bit * count, count
 
-    pending = []
+    def handing(step, frame, giver):
+        return pltpu.make_async_remote_copy(
+            src_ref=sums[levels - 1].at[frame, 0, pl.ds(peers[step][0] * blk_dev, blk_dev)],
+            dst_ref=out.at[giver * frame_dev + frame],
+            send_sem=out_send.at[step, frame],
+            recv_sem=out_recv.at[step, frame],
+            device_id=peers[step],
+            device_id_type=MESH,
+        )
+
+    def prepare(frame):
+        fetch(frame).wait()
+
+        def conv_row(y, carry):
+            wide = jnp.concatenate([padded[frame, y], padded[frame, y + 1], padded[frame, y + 2]], axis=-1)
+            sums_at = jnp.dot(wide, w_cat[...], preferred_element_type=F32)
+            edge = jnp.zeros((1, chans), F32)
+            left = jnp.concatenate([edge, sums_at[: cols - 1, :chans]], axis=0)
+            right = jnp.concatenate([sums_at[1:, 2 * chans :], edge], axis=0)
+            conv[y, :cols] = left + sums_at[:, chans : 2 * chans] + right
+            return carry
+
+        lax.fori_loop(0, rows + 2, conv_row, 0)
+
+        def cut(slot, carry):
+            within = reversed_bits(slot, levels)
+            for group_at in range(n_frames):
+                for extra in range(blk_dev):
+                    block = group_at * per_group + within * blk_dev + extra
+                    first = owners[block] * rows + row_off[frame, block] - REACH
+                    local = first - tile * rows
+                    col = col_off[frame, block]
+                    for i in range(WIN):
+                        row = local + i
+                        there = (row >= -1) & (row <= rows)
+                        there = there & (first + i >= 0) & (first + i < n_tiles * rows)
+                        at = jnp.where(there, row + 1, rows + 2)
+                        win[group_at * blk_dev + extra, i * WIN : (i + 1) * WIN, :] = conv[at, pl.ds(col, WIN), :]
+            parts[frame, slot] = win[...].astype(BF16)
+            return carry
+
+        lax.fori_loop(0, n_tiles, cut, 0)
+
+    def combine(level, frame):
+        copy, source, start, count = halving(level, frame)
+        copy.wait_recv()
+
+        def add(i, carry):
+            both = source[frame, start + i].astype(F32) + lands[level][frame, i].astype(F32)
+            sums[level][frame, i] = both.astype(BF16)
+            return carry
+
+        lax.fori_loop(0, count, add, 0)
+        if level + 1 < levels:
+            halving(level + 1, frame)[0].start()
+        else:
+            for step in range(n_frames - 1):
+                handing(step, frame, group).start()
+            out[group * frame_dev + frame] = sums[level][frame, 0, pl.ds(group * blk_dev, blk_dev)]
+
+    prepare(0)
+    pl.semaphore_wait(barrier, len(partners) + len(peers))
+    halving(0, 0)[0].start()
+
+    def advance(turn, carry):
+        @pl.when(turn < frame_dev)
+        def _():
+            prepare(turn)
+            halving(0, turn)[0].start()
+
+        for level in reversed(range(levels)):
+            frame = turn - 1 - level
+
+            @pl.when((frame >= 0) & (frame < frame_dev))
+            def _():
+                combine(level, frame)
+
+        return carry
+
+    lax.fori_loop(1, frame_dev + levels, advance, 0)
     for frame in range(frame_dev):
-        halving(0, frame)[0].start()
-    for level in range(levels):
-        for frame in range(frame_dev):
-            copy, source, start, count = halving(level, frame)
-            copy.wait_recv()
-            pending.append(copy)
-
-            def add(i, carry):
-                both = source[frame, start + i].astype(F32) + lands[level][frame, i].astype(F32)
-                sums[level][frame, i] = both.astype(BF16)
-                return carry
-
-            lax.fori_loop(0, count, add, 0)
-            if level + 1 < levels:
-                halving(level + 1, frame)[0].start()
-            else:
-                for step, peer in enumerate(peers):
-                    away = pltpu.make_async_remote_copy(
-                        src_ref=sums[level].at[frame, 0, pl.ds(peer[0] * blk_dev, blk_dev)],
-                        dst_ref=out.at[group * frame_dev + frame],
-                        send_sem=out_send.at[step, frame],
-                        recv_sem=out_recv.at[step, frame],
-                        device_id=peer,
-                        device_id_type=MESH,
-                    )
-                    away.start()
-                out[group * frame_dev + frame] = sums[level][frame, 0, pl.ds(group * blk_dev, blk_dev)]
-    for copy in pending:
-        copy.wait_send()
-    for step, peer in enumerate(peers):
-        for frame in range(frame_dev):
-            giver = (group + n_frames - step - 1) % n_frames
-            pltpu.make_async_remote_copy(
-                src_ref=sums[levels - 1].at[frame, 0, pl.ds(peer[0] * blk_dev, blk_dev)],
-                dst_ref=out.at[giver * frame_dev + frame],
-                send_sem=out_send.at[step, frame],
-                recv_sem=out_recv.at[step, frame],
-                device_id=peer,
-                device_id_type=MESH,
-            ).wait()
+        for level in range(levels):
+            halving(level, frame)[0].wait_send()
+        for step in range(n_frames - 1):
+            handing(step, frame, (group + n_frames - step - 1) % n_frames).wait()
 
 
 def rms_scale(values, gain):
@@ -254,41 +257,29 @@
     whole = pl.BlockSpec(memory_space=pltpu.VMEM)
     scalars = pl.BlockSpec(memory_space=pltpu.SMEM)
 
-    w_cat = w_conv.transpose(0, 2, 1, 3).reshape(3 * chans, 3 * chans)
-    parts = pl.pallas_call(
-        functools.partial(window_kernel, n_tiles, n_frames),
-        grid=(frame_dev,),
-        out_shape=jax.ShapeDtypeStruct((frame_dev, n_tiles, lots, CELLS, chans), BF16),
-        in_specs=[
-            scalars,
-            scalars,
-            scalars,
-            pl.BlockSpec((1, rows, cols, chans), lambda f: (f, 0, 0, 0)),
-            pl.BlockSpec((3 * chans, 3 * chans), lambda f: (0, 0)),
-        ],
-        out_specs=pl.BlockSpec((1, n_tiles, lots, CELLS, chans), lambda f: (f, 0, 0, 0, 0)),
-        scratch_shapes=[
-            pltpu.VMEM((rows + 4, cols, chans), BF16),
-            pltpu.VMEM((rows + 2, cols + 16, chans), F32),
-            pltpu.VMEM((CELLS, chans), F32),
-        ],
-    )(owners[:, 0], offset_rows, offset_cols, features, w_cat)
-
     halves = [
         pltpu.VMEM((frame_dev, n_tiles >> (level + 1), lots, CELLS, chans), BF16)
         for level in range(levels)
     ]
     patch = pl.pallas_call(
-        functools.partial(exchange_kernel, n_tiles, n_frames),
+        functools.partial(window_kernel, n_tiles, n_frames),
         out_shape=jax.ShapeDtypeStruct((frames_total, blk_dev, CELLS, chans), BF16),
-        in_specs=[whole],
+        in_specs=[scalars, scalars, scalars, pl.BlockSpec(memory_space=pl.ANY), whole],
         out_specs=whole,
-        scratch_shapes=halves
+        scratch_shapes=[
+            pltpu.VMEM((3 * chans, 3 * chans), BF16),
+            pltpu.VMEM((frame_dev, rows + 4, cols, chans), BF16),
+            pltpu.VMEM((rows + 3, cols + 16, chans), F32),
+            pltpu.VMEM((lots, CELLS, chans), F32),
+            pltpu.VMEM((frame_dev, n_tiles, lots, CELLS, chans), BF16),
+        ]
         + halves
+        + halves
+        + [pltpu.SemaphoreType.DMA((frame_dev,))]
         + [pltpu.SemaphoreType.DMA((levels, frame_dev))] * 2
         + [pltpu.SemaphoreType.DMA((n_frames - 1, frame_dev))] * 2,
         compiler_params=pltpu.CompilerParams(collective_id=0, has_side_effects=True),
-    )(parts)
+    )(owners[:, 0], offset_rows, offset_cols, features, w_conv)
 
     bundle = 4
     span = GROUP * frames_total

time: 117 us -> 105 us (0.90)
  Pallas kernels: 111 us -> 97.6 us
    pallas_call x2 -> x1, Pallas kernels: 68.4 us -> 55 us  [body(): pl.pallas_call(functools.partial(window_kernel, n_tiles, n_frames), out_s...]
    transpose x1 -> x0, local copies, waits for them, and re-layouts: 1.22 us -> none  [body(): w_cat = w_conv.transpose(0, 2, 1, 3).reshape(3 * chans, 3 * chans)]
where the time goes in v2:
time: 105 us
  Pallas kernels  97.6 us (93%)
  local copies, waits for them, and re-layouts  6.86 us (7%)
    pallas_call x1, Pallas kernels, body(): pl.pallas_call(functools.partial(window_kernel, n_tiles, n_frames), out_s...  55 us
    pallas_call x1, Pallas kernels, body(): pl.pallas_call(functools.partial(token_kernel, bundle), grid=(tracks // (...  42.7 us

profile of v2, /device:TPU:0, one launch (start us, length us, event | category | flops | bytes accessed | tf_op | source)
XLA Modules:
  0.0 104.5 jit_solution(1068994104573062752)
XLA Ops:
  0.0 1.3 %broadcast_in_dim.6.gain_attn = f32[1,384]{1,0:T(1,128)} reshape(f32[384]{0:T(512)} %param.26) | data formatting | bytes 3072 | tf_op jit(solution)/shard_map/broadcast_in_dim | solution.py:315
  1.3 1.3 %broadcast_in_dim.7.gain_mlp = f32[1,384]{1,0:T(1,128)} reshape(f32[384]{0:T(512)} %param.29) | data formatting | bytes 3072 | tf_op jit(solution)/shard_map/broadcast_in_dim | solution.py:316
  2.5 0.7 tile.10
  3.3 1.5 %pad.4.w_corr = bf16[96,384]{1,0:T(8,128)(2,1)} pad(bf16[81,384]{1,0:T(8,128)(2,1)} %param.23, bf16[]{:T(256)} %constant.2.clone.1), padding=0_15x0_0 | pad | bytes 135938 | tf_op jit(solution)/shard_map/jit(_pad)/pad | solution.py:289
  4.8 0.7 tile.12.starts
  5.5 0.0 copy-start
  5.5 55.0 %shard_map.154.patch = bf16[16,1,96,128]{3,2,1,0:T(8,128)(2,1)} custom-call(s32[32]{0:T(128)} %bitcast.6, s32[4,32]{1,0:T(4,128)} %row_off.1, s32[4,32]{1,0:T(4,128)} %col_off.1, bf16[4,8,480,128]{3,2,1,0:T(8,128)(2,1)} %feat.1, bf16[3,3,128,128]{3,2,1,0:T(8,128)(2,1)} %w_conv.1), custom_call_target="tpu_custom_call" | custom-call | tf_op jit(solution)/shard_map/pallas_call | solution.py:264
  60.5 0.0 copy-done
  60.5 1.3 %copy.18 = bf16[384,1152]{0,1:T(8,128)(2,1)} copy(bf16[384,1152]{1,0:T(8,128)(2,1)S(1)} %copy-done) | data formatting | bytes 1769472 | tf_op args[11]
  61.8 42.7 %shard_map.155 = bf16[2048,384]{1,0:T(8,128)(2,1)} custom-call(bf16[16,1,96,128]{3,2,1,0:T(8,128)(2,1)} %shard_map.154.patch, bf16[128,128]{1,0:T(8,128)(2,1)} %query.1, s32[4,4,128]{2,1,0:T(4,128)} %tile.12.starts, bf16[96,384]{1,0:T(8,128)(2,1)} %pad.4.w_corr, bf16[128,384]{1,0:T(8,128)(2,1)} %w_feat.1, f32[16,384]{1,0:T(8,128)} %time_embed.1, ...), custom_call_target="tpu_custom_call" | custom-call | tf_op jit(solution)/shard_map/pallas_call | solution.py:294
  (1 shorter events, 0.0 us)
Async XLA Ops:
  5.5 55.0 %copy-start = (bf16[384,1152]{1,0:T(8,128)(2,1)S(1)}, bf16[384,1152]{1,0:T(8,128)(2,1)}, u32[]{:S(2)}) copy-start(bf16[384,1152]{1,0:T(8,128)(2,1)} %param.27) | copy-start | bytes 2654212

commit v3 on v2

--- a/solution.py
+++ b/solution.py
@@ -1,4 +1,5 @@
 import functools
+import math
 
 import jax
 import jax.numpy as jnp
@@ -56,8 +57,10 @@
         padded[frame, 0:2] = blank
         padded[frame, rows + 2 : rows + 4] = blank
     win[...] = jnp.zeros_like(win)
-    conv[rows + 2] = jnp.zeros(conv.shape[1:], F32)
-    conv[:, cols:] = jnp.zeros((rows + 3, conv.shape[1] - cols, chans), F32)
+    for y in range(WIN):
+        conv[y] = jnp.zeros(conv.shape[1:], F32)
+        conv[WIN + rows + 2 + y] = jnp.zeros(conv.shape[1:], F32)
+    conv[WIN : WIN + rows + 2, cols:] = jnp.zeros((rows + 2, conv.shape[1] - cols, chans), F32)
     for a in range(3):
         for b in range(3):
             w_cat[a * chans : (a + 1) * chans, b * chans : (b + 1) * chans] = w_conv[a, b]
@@ -89,31 +92,38 @@
     def prepare(frame):
         fetch(frame).wait()
 
-        def conv_row(y, carry):
-            wide = jnp.concatenate([padded[frame, y], padded[frame, y + 1], padded[frame, y + 2]], axis=-1)
-            sums_at = jnp.dot(wide, w_cat[...], preferred_element_type=F32)
-            edge = jnp.zeros((1, chans), F32)
-            left = jnp.concatenate([edge, sums_at[: cols - 1, :chans]], axis=0)
-            right = jnp.concatenate([sums_at[1:, 2 * chans :], edge], axis=0)
-            conv[y, :cols] = left + sums_at[:, chans : 2 * chans] + right
+        def conv_rows(pair, carry):
+            for half in range(2):
+                y = 2 * pair + half
+                wide = jnp.concatenate([padded[frame, y], padded[frame, y + 1], padded[frame, y + 2]], axis=-1)
+                sums_at = jnp.dot(wide, w_cat[...], preferred_element_type=F32)
+                edge = jnp.zeros((1, chans), F32)
+                left = jnp.concatenate([edge, sums_at[: cols - 1, :chans]], axis=0)
+                right = jnp.concatenate([sums_at[1:, 2 * chans :], edge], axis=0)
+                conv[WIN + y, :cols] = left + sums_at[:, chans : 2 * chans] + right
             return carry
 
-        lax.fori_loop(0, rows + 2, conv_row, 0)
+        lax.fori_loop(0, (rows + 2) // 2, conv_rows, 0)
+
+        @pl.when(tile == 0)
+        def _():
+            conv[WIN, :cols] = jnp.zeros((cols, chans), F32)
+
+        @pl.when(tile == n_tiles - 1)
+        def _():
+            conv[WIN + rows + 1, :cols] = jnp.zeros((cols, chans), F32)
 
         def cut(slot, carry):
             within = reversed_bits(slot, levels)
             for group_at in range(n_frames):
                 for extra in range(blk_dev):
                     block = group_at * per_group + within * blk_dev + extra
-                    first = owners[block] * rows + row_off[frame, block] - REACH
-                    local = first - tile * rows
+                    local = (owners[block] - tile) * rows + row_off[frame, block] - REACH
+                    first = jnp.clip(local + 1, -WIN, rows + 2) + WIN
                     col = col_off[frame, block]
+                    lot = group_at * blk_dev + extra
                     for i in range(WIN):
-                        row = local + i
-                        there = (row >= -1) & (row <= rows)
-                        there = there & (first + i >= 0) & (first + i < n_tiles * rows)
-                        at = jnp.where(there, row + 1, rows + 2)
-                        win[group_at * blk_dev + extra, i * WIN : (i + 1) * WIN, :] = conv[at, pl.ds(col, WIN), :]
+                        win[lot, i * WIN : (i + 1) * WIN, :] = conv[first + i, pl.ds(col, WIN), :]
             parts[frame, slot] = win[...].astype(BF16)
             return carry
 
@@ -168,29 +178,38 @@
 
 
 def token_kernel(
-    bundle, patch, query, starts, w_corr, w_feat, time_embed, gain_attn, w_qkv_t, w_attn_out, gain_mlp,
-    w_up, w_down, out, tokens,
+    bundle, patch, query, starts, w_corr, w_feat, time_embed, gain_attn, w_qkv, w_attn_out, gain_mlp,
+    w_up, w_down, out, tokens, w_token, w_qkv_t,
 ):
     step = pl.program_id(0)
-    frames = patch.shape[0]
-    chans = query.shape[1]
+    frames, _, cells, chans = patch.shape
     width = w_feat.shape[1]
     head = width // HEADS
     span = GROUP * frames
     per_block = QBLK // (GROUP * bundle)
 
+    @pl.when(step == 0)
+    def _():
+        w_token[:chans] = jnp.zeros((chans, width), BF16)
+        w_token[: w_corr.shape[0]] = w_corr[...]
+        w_token[chans:] = w_feat[...]
+        w_qkv_t[...] = w_qkv[...].T
+
     @pl.when(step % per_block == 0)
     def _():
         queries = query[...]
-        feat = jnp.dot(queries, w_feat[...], preferred_element_type=F32)
-        for frame in range(frames):
-            corr = lax.dot_general(
-                patch[frame, 0], queries, (((1,), (1,)), ((), ())), preferred_element_type=F32
-            ) * chans ** (-0.5)
-            part = lax.dot_general(
-                corr.astype(BF16), w_corr[...], (((0,), (0,)), ((), ())), preferred_element_type=F32
-            )
-            tokens[frame] = part + feat + time_embed[frame : frame + 1, :]
+        blank = jnp.zeros((chans - cells, chans), BF16)
+        for some in range(0, frames, 4):
+            corrs = []
+            for frame in range(some, some + 4):
+                window = jnp.concatenate([patch[frame, 0], blank], axis=0)
+                corr = lax.dot_general(
+                    queries, window, (((1,), (1,)), ((), ())), preferred_element_type=F32
+                ) * chans ** (-0.5)
+                corrs.append(jnp.concatenate([corr.astype(BF16), queries], axis=1))
+            made = jnp.dot(jnp.concatenate(corrs, axis=0), w_token[...], preferred_element_type=F32)
+            for n in range(4):
+                tokens[some + n] = made[n * QBLK : (n + 1) * QBLK] + time_embed[some + n : some + n + 1, :]
 
     first = (step % per_block) * (GROUP * bundle)
     x = jnp.concatenate(
@@ -207,24 +226,42 @@
     key_at = lax.broadcasted_iota(jnp.int32, (span, span), 0)
     query_at = lax.broadcasted_iota(jnp.int32, (span, span), 1)
     same = (key_at % GROUP) == (query_at % GROUP)
+    power = head ** (-0.5) * math.log2(math.e)
+    start_rows = jnp.broadcast_to(starts[...].astype(F32)[None, :], (GROUP, QBLK)).astype(BF16)
+    source = lax.broadcasted_iota(jnp.int32, (QBLK, span), 0)
+    track = lax.broadcasted_iota(jnp.int32, (QBLK, span), 1) % GROUP
     gathered = []
     for g in range(bundle):
         at = slice(g * span, (g + 1) * span)
-        valid = same & ((key_at // GROUP) >= starts[0, g : g + 1, :])
-        heads = []
+        pick = (source == track + (first + GROUP * g)).astype(BF16)
+        start = jnp.dot(start_rows, pick, preferred_element_type=F32)[:1].astype(jnp.int32)
+        valid = same & ((key_at // GROUP) >= start)
+        scores = [
+            lax.dot_general(
+                qkv[width + h * head : width + (h + 1) * head, at],
+                qkv[h * head : (h + 1) * head, at],
+                (((0,), (0,)), ((), ())),
+                preferred_element_type=F32,
+            )
+            for h in range(HEADS)
+        ]
+        weights, totals = [], []
         for h in range(HEADS):
-            query_h = qkv[h * head : (h + 1) * head, at]
-            key_h = qkv[width + h * head : width + (h + 1) * head, at]
-            value_h = qkv[2 * width + h * head : 2 * width + (h + 1) * head, at]
-            scores = lax.dot_general(
-                key_h, query_h, (((0,), (0,)), ((), ())), preferred_element_type=F32
-            ) * head ** (-0.5)
-            scores = jnp.where(valid, scores, -1e30)
-            weights = jnp.exp(scores - jnp.max(scores, axis=0, keepdims=True))
-            total = jnp.sum(weights, axis=0, keepdims=True)
-            mixed_h = jnp.dot(value_h, weights.astype(BF16), preferred_element_type=F32)
-            heads.append((mixed_h / total).astype(BF16))
-        gathered.append(jnp.concatenate(heads, axis=0))
+            score = jnp.where(valid, scores[h], -1e30)
+            weight = jnp.exp2((score - jnp.max(score, axis=0, keepdims=True)) * power)
+            totals.append(jnp.sum(weight, axis=0, keepdims=True))
+            weights.append(weight.astype(BF16))
+        heads = [
+            jnp.dot(
+                qkv[2 * width + h * head : 2 * width + (h + 1) * head, at],
+                weights[h],
+                preferred_element_type=F32,
+            )
+            for h in range(HEADS)
+        ]
+        gathered.append(
+            jnp.concatenate([(heads[h] / totals[h]).astype(BF16) for h in range(HEADS)], axis=0)
+        )
     attended = jnp.concatenate(gathered, axis=1)
     mixed = x + lax.dot_general(
         attended, w_attn_out[...], (((0,), (0,)), ((), ())), preferred_element_type=F32
@@ -269,7 +306,7 @@
         scratch_shapes=[
             pltpu.VMEM((3 * chans, 3 * chans), BF16),
             pltpu.VMEM((frame_dev, rows + 4, cols, chans), BF16),
-            pltpu.VMEM((rows + 3, cols + 16, chans), F32),
+            pltpu.VMEM((rows + 2 + 2 * WIN, cols + 16, chans), F32),
             pltpu.VMEM((lots, CELLS, chans), F32),
             pltpu.VMEM((frame_dev, n_tiles, lots, CELLS, chans), BF16),
         ]
@@ -285,9 +322,6 @@
     span = GROUP * frames_total
     tracks = blk_dev * QBLK
     per_block = QBLK // (GROUP * bundle)
-    starts = jnp.tile(start_frames.reshape(-1, bundle, GROUP), (1, 1, frames_total))
-    w_corr_pad = jnp.pad(w_corr, ((0, CELLS - WIN * WIN), (0, 0)))
-
     def fixed(shape):
         return pl.BlockSpec(shape, lambda s: (0,) * len(shape))
 
@@ -298,22 +332,26 @@
         in_specs=[
             pl.BlockSpec((frames_total, 1, CELLS, chans), lambda s: (0, s // per_block, 0, 0)),
             pl.BlockSpec((QBLK, chans), lambda s: (s // per_block, 0)),
-            pl.BlockSpec((1, bundle, span), lambda s: (s, 0, 0)),
-            fixed((CELLS, width)),
+            pl.BlockSpec((QBLK,), lambda s: (s // per_block,)),
+            fixed(w_corr.shape),
             fixed(w_feat.shape),
             fixed(time_embed.shape),
-            fixed((1, width)),
-            fixed((3 * width, width)),
+            fixed((width,)),
+            fixed(w_qkv.shape),
             fixed(w_attn_out.shape),
-            fixed((1, width)),
+            fixed((width,)),
             fixed(w_up.shape),
             fixed(w_down.shape),
         ],
         out_specs=pl.BlockSpec((bundle * span, width), lambda s: (s, 0)),
-        scratch_shapes=[pltpu.VMEM((frames_total, QBLK, width), F32)],
+        scratch_shapes=[
+            pltpu.VMEM((frames_total, QBLK, width), F32),
+            pltpu.VMEM((2 * chans, width), BF16),
+            pltpu.VMEM((3 * width, width), BF16),
+        ],
     )(
-        patch, query_feats, starts, w_corr_pad, w_feat, time_embed, gain_attn[None], w_qkv.T,
-        w_attn_out, gain_mlp[None], w_up, w_down,
+        patch, query_feats, start_frames, w_corr, w_feat, time_embed, gain_attn, w_qkv,
+        w_attn_out, gain_mlp, w_up, w_down,
     )
     return refined.reshape(tracks, frames_total, width)
 

time: 105 us -> 72.9 us (0.69)
  Pallas kernels: 97.6 us -> 72.8 us
  local copies, waits for them, and re-layouts: 6.86 us -> 0 us
    pallas_call x1, Pallas kernels: 42.7 us -> 22.8 us  [body(): pl.pallas_call(functools.partial(token_kernel, bundle), grid=(tracks // (...]
    pallas_call x1, Pallas kernels: 55 us -> 50 us  [body(): pl.pallas_call(functools.partial(window_kernel, n_tiles, n_frames), out_s...]
    broadcast_in_dim x2 -> x0, local copies, waits for them, and re-layouts: 2.53 us -> none  [the longest x1 1.27 us: body(): gain_mlp[None]]
    pad x1 -> x0, local copies, waits for them, and re-layouts: 1.52 us -> none  [body(): w_corr_pad = jnp.pad(w_corr, ((0, CELLS - WIN * WIN), (0, 0)))]
    another operation x3 -> x0, local copies, waits for them, and re-layouts: 1.46 us -> none  [body(): jnp.tile(start_frames.reshape(-1, bundle, GROUP), (1, 1, frames_total))]
    unnamed x3 -> x0, local copies, waits for them, and re-layouts: 1.35 us -> none
where the time goes in v3:
time: 72.9 us; the launch traced here: 72.8 us
  Pallas kernels  72.8 us (100%)
    pallas_call x1, Pallas kernels, body(): pl.pallas_call(functools.partial(window_kernel, n_tiles, n_frames), out_s...  50 us
    pallas_call x1, Pallas kernels, body(): pl.pallas_call(functools.partial(token_kernel, bundle), grid=(tracks // (...  22.8 us

profile of v3, /device:TPU:0, one launch (start us, length us, event | category | flops | bytes accessed | tf_op | source)
XLA Modules:
  0.0 72.8 jit_solution(1089890520631441577)
XLA Ops:
  0.0 50.0 %shard_map.154.patch = bf16[16,1,96,128]{3,2,1,0:T(8,128)(2,1)} custom-call(s32[32]{0:T(128)} %bitcast.2, s32[4,32]{1,0:T(4,128)} %row_off.1, s32[4,32]{1,0:T(4,128)} %col_off.1, bf16[4,8,480,128]{3,2,1,0:T(8,128)(2,1)} %feat.1, bf16[3,3,128,128]{3,2,1,0:T(8,128)(2,1)} %w_conv.1), custom_call_target="tpu_custom_call" | custom-call | tf_op jit(solution)/shard_map/pallas_call | solution.py:301
  50.0 22.8 %shard_map.155 = bf16[2048,384]{1,0:T(8,128)(2,1)} custom-call(bf16[16,1,96,128]{3,2,1,0:T(8,128)(2,1)} %shard_map.154.patch, bf16[128,128]{1,0:T(8,128)(2,1)} %query.1, s32[128]{0:T(128)} %starts.1, bf16[81,384]{1,0:T(8,128)(2,1)} %w_corr.1, bf16[128,384]{1,0:T(8,128)(2,1)} %w_feat.1, f32[16,384]{1,0:T(8,128)} %time_embed.1, f32[384]{0:T(512)} %gain_attn.1, ...), custom_call_target="tpu_custom_call" | custom-call | tf_op jit(solution)/shard_map/pallas_call | solution.py:328

commit v4 on v3

--- a/solution.py
+++ b/solution.py
@@ -11,7 +11,7 @@
 HEADS = 8
 WIN = 9
 QBLK = 128
-CELLS = 96
+CELLS = 88
 REACH = WIN // 2
 GROUP = 8
 F32 = jnp.float32
@@ -89,7 +89,7 @@
             device_id_type=MESH,
         )
 
-    def prepare(frame):
+    def convolve(frame):
         fetch(frame).wait()
 
         def conv_rows(pair, carry):
@@ -113,6 +113,7 @@
         def _():
             conv[WIN + rows + 1, :cols] = jnp.zeros((cols, chans), F32)
 
+    def cut_all(frame):
         def cut(slot, carry):
             within = reversed_bits(slot, levels)
             for group_at in range(n_frames):
@@ -146,17 +147,26 @@
                 handing(step, frame, group).start()
             out[group * frame_dev + frame] = sums[level][frame, 0, pl.ds(group * blk_dev, blk_dev)]
 
-    prepare(0)
+    convolve(0)
+    cut_all(0)
     pl.semaphore_wait(barrier, len(partners) + len(peers))
     halving(0, 0)[0].start()
 
     def advance(turn, carry):
         @pl.when(turn < frame_dev)
         def _():
-            prepare(turn)
+            convolve(turn)
+
+        @pl.when(turn <= frame_dev)
+        def _():
+            combine(0, turn - 1)
+
+        @pl.when(turn < frame_dev)
+        def _():
+            cut_all(turn)
             halving(0, turn)[0].start()
 
-        for level in reversed(range(levels)):
+        for level in reversed(range(1, levels)):
             frame = turn - 1 - level
 
             @pl.when((frame >= 0) & (frame < frame_dev))

time: 72.9 us -> 67.3 us (0.923)
  Pallas kernels: 72.8 us -> 67.1 us
    pallas_call x1, Pallas kernels: 50 us -> 44.3 us  [body(): pl.pallas_call(functools.partial(window_kernel, n_tiles, n_frames), out_s...]
where the time goes in v4:
time: 67.3 us; the launch traced here: 67.1 us
  Pallas kernels  67.1 us (100%)
    pallas_call x1, Pallas kernels, body(): pl.pallas_call(functools.partial(window_kernel, n_tiles, n_frames), out_s...  44.3 us
    pallas_call x1, Pallas kernels, body(): pl.pallas_call(functools.partial(token_kernel, bundle), grid=(tracks // (...  22.8 us

profile of v4, /device:TPU:0, one launch (start us, length us, event | category | flops | bytes accessed | tf_op | source)
XLA Modules:
  0.0 67.1 jit_solution(811470303994260259)
XLA Ops:
  0.0 44.3 %shard_map.154.patch = bf16[16,1,88,128]{3,2,1,0:T(8,128)(2,1)} custom-call(s32[32]{0:T(128)} %bitcast.2, s32[4,32]{1,0:T(4,128)} %row_off.1, s32[4,32]{1,0:T(4,128)} %col_off.1, bf16[4,8,480,128]{3,2,1,0:T(8,128)(2,1)} %feat.1, bf16[3,3,128,128]{3,2,1,0:T(8,128)(2,1)} %w_conv.1), custom_call_target="tpu_custom_call" | custom-call | tf_op jit(solution)/shard_map/pallas_call | solution.py:311
  44.3 22.8 %shard_map.155 = bf16[2048,384]{1,0:T(8,128)(2,1)} custom-call(bf16[16,1,88,128]{3,2,1,0:T(8,128)(2,1)} %shard_map.154.patch, bf16[128,128]{1,0:T(8,128)(2,1)} %query.1, s32[128]{0:T(128)} %starts.1, bf16[81,384]{1,0:T(8,128)(2,1)} %w_corr.1, bf16[128,384]{1,0:T(8,128)(2,1)} %w_feat.1, f32[16,384]{1,0:T(8,128)} %time_embed.1, f32[384]{0:T(512)} %gain_attn.1, ...), custom_call_target="tpu_custom_call" | custom-call | tf_op jit(solution)/shard_map/pallas_call | solution.py:338
